TPU v7x, 32 devices: a whole 2x2x4 slice. The times are simulated.
32 devices in a mesh: var: 8 (over y, x, core), samp: 4 (over z).
Axes of the slice: x: 2, y: 2, z: 4, core: 2. Of those that a mesh axis runs over, the one named last changes fastest.
Arguments:
- dosages: bfloat16 [16384, 4096], P('samp', 'var'), as said below
- window_end: int32 [4096], P('var'), may hold values from 0 to 4095, as said below
Outputs:
- correlations: bfloat16 [4096, 2048], P('var')
Inputs may be any that keep to these rules, and one draw needn't show every extreme that they name: For a variant in block b (of 512 variants), window_end lies in block b + 1, b + 2 or b + 3 (the same block reach for the whole block), clipped to 4095; some variant reaches the last variant of the block three ahead. `dosages`: dosages lie between 0 and 2.
All inputs are finite; a program needn't handle non-finite values.
Results may differ from a plain program's by a relative error of at most 0.0034.
Values may be sent and summed in bfloat16 or wider, within the bound.
A program may use at most 64 MiB of HBM per device.

v0:
```python
import jax
import jax.numpy as jnp
from jax import lax
from jax.sharding import PartitionSpec as P


def passed_along(value, axis, steps):
    count = lax.axis_size(axis)
    first, last = (max(0, -steps), min(count, count - steps))
    return lax.ppermute(value, axis, [(source, source + steps) for source in range(first, last)])


def per_device(dosages, window_end):
    local_rows = dosages.shape[0]
    width = dosages.shape[1]
    groups = lax.axis_size("samp")
    total = local_rows * groups
    data = dosages.astype(jnp.float32)
    sums, squares = lax.psum((jnp.sum(data, axis=0), jnp.sum(data * data, axis=0)), "samp")
    mean = sums / total
    spread = 1.0 / jnp.sqrt(squares / total - mean * mean + 1e-05)
    standard = ((data - mean[None, :]) * spread[None, :]).astype(jnp.bfloat16)
    pieces = [standard]
    for step in range(1, 4):
        pieces.append(passed_along(standard, "var", -step))
    band = jnp.concatenate(pieces, axis=1)
    block_start = lax.axis_index("var") * width
    columns = jnp.arange(4 * width, dtype=jnp.int32)
    share = width // groups
    mine = lax.psum_scatter(
        jnp.einsum("sa,sb->ab", standard, band, preferred_element_type=jnp.float32),
        "samp",
        scatter_dimension=0,
        tiled=True,
    )
    ends = lax.dynamic_slice_in_dim(window_end, lax.axis_index("samp") * share, share, 0)
    target = block_start + columns
    keep = (columns[None, :] < width) | (target[None, :] <= ends[:, None])
    return lax.all_gather(
        jnp.where(keep, mine / total, 0.0).astype(jnp.bfloat16), "samp", axis=0, tiled=True
    )


def solution(mesh):
    placed = (P("samp", "var"), P("var"))
    return jax.shard_map(
        per_device, mesh=mesh, in_specs=placed, out_specs=P("var", None), check_vma=False
    )
```

profile of v0, /device:TPU:26, one launch (start us, length us, event | category | flops | bytes accessed | tf_op | source)
XLA Modules:
  0.0 395.5 jit_solution(911435030028375783)
XLA Ops:
  6.5 0.0 reduce-scatter.2.cloned.1.call-start
  6.5 3.3 convert_reduce_fusion
  9.9 8.2 %all-reduce = (f32[512]{0:T(512)S(1)}, f32[512]{0:T(512)S(1)}) all-reduce(f32[512]{0:T(512)S(1)} %get-tuple-element.6, f32[512]{0:T(512)S(1)} %get-tuple-element.5), channel_id=1, replica_groups=mesh['var'=8,'samp'=4] {'samp'}, use_global_device_ids=true, to_apply=%region_3.0 | all-reduce | flops 1024 | bytes 8192 | tf_op jit(solution)/shard_map/psum | solution.py:19
  18.0 3.2 fusion.9
  21.3 1.9 collective-permute-start
  23.2 1.9 collective-permute-start.1
  25.1 1.5 collective-permute-start.2
  26.6 85.6 %collective-permute-done = bf16[4096,512]{1,0:T(8,128)(2,1)S(1)} collective-permute-done((bf16[4096,512]{1,0:T(8,128)(2,1)S(1)}, bf16[4096,512]{1,0:T(8,128)(2,1)S(1)}, u32[]{:S(2)}, u32[]{:S(2)}) %collective-permute-start) | collective-permute-done | bytes 4194336 | tf_op jit(solution)/shard_map/ppermute | solution.py:10
  112.2 91.0 %collective-permute-done.1 = bf16[4096,512]{1,0:T(8,128)(2,1)S(1)} collective-permute-done((bf16[4096,512]{1,0:T(8,128)(2,1)S(1)}, bf16[4096,512]{1,0:T(8,128)(2,1)S(1)}, u32[]{:S(2)}, u32[]{:S(2)}) %collective-permute-start.1) | collective-permute-done | bytes 4194336 | tf_op jit(solution)/shard_map/ppermute | solution.py:10
  203.2 2.9 collective-permute-done.2
  206.1 10.8 %fusion = f32[512,2048]{1,0:T(8,128)} fusion(bf16[4096,512]{1,0:T(8,128)(2,1)S(1)} %fusion.9, bf16[4096,512]{1,0:T(8,128)(2,1)S(1)} %collective-permute-done.2, bf16[4096,512]{1,0:T(8,128)(2,1)S(1)} %collective-permute-done.1, bf16[4096,512]{1,0:T(8,128)(2,1)S(1)} %collective-permute-done), kind=kOutput, calls=%fused_computation | convolution fusion | flops 8657043456 | bytes 20971520 | tf_op jit(solution)/shard_map/sa,sb->ab/dot_general | solution.py:31
  216.9 0.0 reduce-scatter.2.cloned.1.call-update
  216.9 0.0 all-gather.2.cloned.1.call-start
  217.0 0.8 dynamic_slice.3
  217.8 120.8 %reduce-scatter.2.cloned.1.call-done = f32[128,2048]{1,0:T(8,128)} async-done(((f32[512,2048]{1,0:T(8,128)}), f32[128,2048]{1,0:T(8,128)}) %reduce-scatter.2.cloned.1.call-update) | async-done | bytes 1048592 | tf_op jit(solution)/shard_map/reduce_scatter | solution.py:30
  338.6 2.3 select_convert_fusion
  340.9 0.0 all-gather.2.cloned.1.call-update
  340.9 44.7 %all-gather.2.cloned.1.call-done = bf16[512,2048]{1,0:T(8,128)(2,1)} async-done(((bf16[128,2048]{1,0:T(8,128)(2,1)}), bf16[512,2048]{1,0:T(8,128)(2,1)}) %all-gather.2.cloned.1.call-update) | async-done | bytes 2097168 | tf_op jit(solution)/shard_map/all_gather | solution.py:39
  385.5 3.2 copy.4
  (3 shorter events, 0.0 us)
Async XLA Ops:
  6.5 332.0 %reduce-scatter.2.cloned.1.call-start = ((), (), s32[]{:S(2)}) async-start(), calls=%async_computation.1 | async-start | bytes 5242880 | tf_op jit(solution)/shard_map/reduce_scatter | solution.py:30
  21.3 90.9 %collective-permute-start = (bf16[4096,512]{1,0:T(8,128)(2,1)S(1)}, bf16[4096,512]{1,0:T(8,128)(2,1)S(1)}, u32[]{:S(2)}, u32[]{:S(2)}) collective-permute-start(bf16[4096,512]{1,0:T(8,128)(2,1)S(1)} %fusion.9), channel_id=1, source_target_pairs={{4,0},{8,4},{12,8},{16,12},{20,16},{24,20},{28,24},{5,1},{9,5},{13... | collective-permute-start | bytes 12582920 | tf_op jit(solution)/shard_map/ppermute | solution.py:10
  23.2 180.0 %collective-permute-start.1 = (bf16[4096,512]{1,0:T(8,128)(2,1)S(1)}, bf16[4096,512]{1,0:T(8,128)(2,1)S(1)}, u32[]{:S(2)}, u32[]{:S(2)}) collective-permute-start(bf16[4096,512]{1,0:T(8,128)(2,1)S(1)} %fusion.9), channel_id=1, source_target_pairs={{8,0},{12,4},{16,8},{20,12},{24,16},{28,20},{9,1},{13,5},{17,9},{2... | collective-permute-start | bytes 12582920 | tf_op jit(solution)/shard_map/ppermute | solution.py:10
  25.1 180.9 %collective-permute-start.2 = (bf16[4096,512]{1,0:T(8,128)(2,1)S(1)}, bf16[4096,512]{1,0:T(8,128)(2,1)S(1)}, u32[]{:S(2)}, u32[]{:S(2)}) collective-permute-start(bf16[4096,512]{1,0:T(8,128)(2,1)S(1)} %fusion.9), channel_id=1, source_target_pairs={{12,0},{16,4},{20,8},{24,12},{28,16},{13,1},{17,5},{21,9},{25,13},... | collective-permute-start | bytes 12582920 | tf_op jit(solution)/shard_map/ppermute | solution.py:10
  216.9 168.6 %all-gather.2.cloned.1.call-start = ((), (), s32[]{:S(2)}) async-start(), calls=%async_computation.2 | async-start | bytes 2621440 | tf_op jit(solution)/shard_map/all_gather | solution.py:39
Sparse Core Ops, SparseCore 0:
  217.1 121.4 reduce-scatter.1
  341.0 44.4 all-gather.1
where the time goes:
time: 400 us; the launch traced here: 396 us
  waiting for transfers between devices  345 us (86%)
  between operations  13.4 us (3%)
  matrix products  10.8 us (3%)
  other arithmetic  8.9 us (2%)
  blocking collectives  8.15 us (2%)
  starting transfers between devices  5.36 us (1%)
    ppermute x3, waiting for transfers between devices, passed_along(): lax.ppermute(value, axis, [(source, source + steps) for source in range(f...  179 us
    reduce_scatter x1, waiting for transfers between devices, per_device(): lax.psum_scatter(jnp.einsum('sa,sb->ab', standard, band, preferred_elemen...  121 us
    all_gather x1, waiting for transfers between devices, per_device(): lax.all_gather(jnp.where(keep, mine / total, 0.0).astype(jnp.bfloat16), '...  44.7 us
    dot_general x1, matrix products, per_device(): jnp.einsum('sa,sb->ab', standard, band, preferred_element_type=jnp.float32)  10.8 us
    psum x1, blocking collectives, per_device(): lax.psum((jnp.sum(data, axis=0), jnp.sum(data * data, axis=0)), 'samp')  8.15 us
  transfers between devices with their start and end apart: 5, of which 5 were waited for; matrix products, arithmetic and copies ran while one was open for 0% of the time, Pallas kernels for 0%

commit v1 on v0

v1 whole, which is shorter than its diff:
```python
import functools

import jax
import jax.numpy as jnp
from jax import lax
from jax.experimental import pallas as pl
from jax.experimental.pallas import tpu as pltpu
from jax.sharding import PartitionSpec as P

MESH = pl.DeviceIdType.MESH
REACH = 4
PARTS = 4
SUBS = 4


def kernel(
    total, nv, ns, data, out, x, xt, other, stat, mine, give, got, arrived, result,
    stat_send, stat_recv, swap_send, swap_recv, near_send, far_send, pass_send, third_send,
    near_recv, far_recv, third_recv, give_send, give_recv,
    sum_send, sum_recv, back_send, back_recv, out_sem,
):
    v = lax.axis_index("var")
    s = lax.axis_index("samp")
    rows, width = data.shape
    half = rows // 2
    chips = nv // 2
    c = v // 2
    j = v % 2
    tile = min(256, half)
    part = half // PARTS

    def dev(chip, core, group):
        return {"var": chip * 2 + core, "samp": group}

    def remote(src, dst, send, recv, where):
        return pltpu.make_async_remote_copy(
            src_ref=src, dst_ref=dst, send_sem=send, recv_sem=recv,
            device_id=where, device_id_type=MESH,
        )

    barrier = pltpu.get_barrier_semaphore()

    def greet(where):
        pl.semaphore_signal(barrier, inc=1, device_id=where, device_id_type=MESH)

    greet(dev(c, 1 - j, s))
    for off in range(1, ns):
        greet(dev(c, j, lax.rem(s + off, ns)))
    for off in (-2, -1, 1, 2):
        @pl.when((c + off >= 0) & (c + off < chips))
        def _():
            greet(dev(c + off, j, s))

    def add_up(i, carry):
        a, b = carry
        d = data[pl.ds(pl.multiple_of(i * tile, tile), tile), :].astype(jnp.float32)
        d = d.reshape(tile // 8, 8, width)
        return a + jnp.sum(d, axis=0), b + jnp.sum(d * d, axis=0)

    zero = jnp.zeros((8, width), jnp.float32)
    a, b = lax.fori_loop(0, rows // tile, add_up, (zero, zero))
    stat[s, 0:1, :] = jnp.sum(a, axis=0, keepdims=True)
    stat[s, 1:2, :] = jnp.sum(b, axis=0, keepdims=True)

    peers = jnp.int32(ns)
    for off in (-2, -1, 1, 2):
        peers = peers + ((c + off >= 0) & (c + off < chips)).astype(jnp.int32)
    pl.semaphore_wait(barrier, peers)

    def stat_out(off):
        return remote(stat.at[s], stat.at[s], stat_send.at[off], stat_recv.at[s],
                      dev(c, j, lax.rem(s + off, ns)))

    for off in range(1, ns):
        stat_out(off).start()
    for off in range(1, ns):
        src = lax.rem(s + off, ns)
        remote(stat.at[src], stat.at[src], stat_send.at[off], stat_recv.at[src],
               dev(c, j, src)).wait_recv()
    sums = stat[0, 0:1, :]
    squares = stat[0, 1:2, :]
    for g in range(1, ns):
        sums = sums + stat[g, 0:1, :]
        squares = squares + stat[g, 1:2, :]
    mean = sums / total
    spread = 1.0 / jnp.sqrt(squares / total - mean * mean + 1e-05)

    def standard(start):
        d = data[pl.ds(pl.multiple_of(start, tile), tile), :].astype(jnp.float32)
        return ((d - mean) * spread).astype(jnp.bfloat16)

    @pl.loop(0, half // tile)
    def _(i):
        at = pl.multiple_of(i * tile, tile)
        other[pl.ds(at, tile), :] = standard((1 - j) * half + at)

    swap = remote(other, x.at[j], swap_send, swap_recv, dev(c, 1 - j, s))
    swap.start()

    @pl.loop(0, half // tile)
    def _(i):
        at = pl.multiple_of(i * tile, tile)
        x[j, pl.ds(at, tile), :] = standard(j * half + at)

    for slot, reach in ((2, 1), (3, 1), (4, 2)):
        @pl.when(c + reach >= chips)
        def _():
            @pl.loop(0, half // tile)
            def _(i):
                at = pl.multiple_of(i * tile, tile)
                x[slot, pl.ds(at, tile), :] = jnp.zeros((tile, width), jnp.bfloat16)

    remote(other, x.at[1 - j], swap_send, swap_recv, dev(c, 1 - j, s)).wait_recv()

    def piece(slot, q):
        return x.at[slot, pl.ds(q * part, part), :]

    def near(q):
        return remote(piece(0, q), piece(2, q), near_send.at[q], near_recv.at[q], dev(c - 1, j, s))

    def far(q):
        return remote(piece(0, q), piece(4, q), far_send.at[q], far_recv.at[q], dev(c - 2, j, s))

    def passed(q):
        return remote(piece(4, q), piece(2, q), pass_send.at[q], near_recv.at[q], dev(c + 1, j, s))

    def third():
        return remote(x.at[1], x.at[3], third_send, third_recv, dev(c - 1, j, s))

    odd = c % 2 == 1
    has_far = c >= 2
    has_near = (c >= 1) & odd
    relays = (c % 2 == 0) & (c + 2 < chips)

    @pl.when(has_far)
    def _():
        for q in range(PARTS):
            far(q).start()

    @pl.when(has_near)
    def _():
        for q in range(PARTS):
            near(q).start()

    @pl.when(c >= 1)
    def _():
        third().start()

    def take_far(q):
        @pl.when(c + 2 < chips)
        def _():
            remote(piece(0, q), piece(4, q), far_send.at[q], far_recv.at[q],
                   dev(c + 2, j, s)).wait_recv()

        @pl.when(relays)
        def _():
            passed(q).start()

    def take_near():
        @pl.when(c + 1 < chips)
        def _():
            for q in range(PARTS):
                remote(piece(0, q), piece(2, q), near_send.at[q], near_recv.at[q],
                       dev(c + 1, j, s)).wait_recv()

    def take_third():
        @pl.when(c + 1 < chips)
        def _():
            remote(x.at[1], x.at[3], third_send, third_recv, dev(c + 1, j, s)).wait_recv()

    for r in range(2):
        @pl.loop(0, half // tile)
        def _(i):
            at = pl.multiple_of(i * tile, tile)
            xt[r, :, pl.ds(at, tile)] = x[r, pl.ds(at, tile), :].T

    side = min(256, width)
    slots = ((0, 1), (1, 2), (2, 4), (3, 3))
    column = ((0, 0), (1, 1), (2, 3), (3, 2))

    def pick(pair, r):
        return pair[0] + r * (pair[1] - pair[0])

    def product(t, r, into):
        slot = pick(slots[t], r)

        @pl.loop(0, (width // side) ** 2)
        def _(i):
            top = pl.multiple_of((i // (width // side)) * side, side)
            left = pl.multiple_of((i % (width // side)) * side, side)
            into[t, pl.ds(top, side), pl.ds(left, side)] = jnp.dot(
                xt[r, pl.ds(top, side), :], x[slot, :, pl.ds(left, side)],
                preferred_element_type=jnp.float32,
            )

    def gave(t):
        return remote(give.at[t], got.at[t], give_send.at[t], give_recv.at[t], dev(c, 1 - j, s))

    def grams(t):
        product(t, 1 - j, give)
        gave(t).start()
        product(t, j, mine)
        gave(t).wait_recv()

    block = width // 2 // SUBS

    def chain(n):
        way = n % 2
        u = n // 2
        lines = pl.ds(pl.multiple_of(way * (width // 2) + u * block, block), block)
        first = s == way * (ns - 1)
        last = s == (1 - way) * (ns - 1)
        step = 1 - 2 * way
        return lines, first, last, step

    def place(t):
        return pl.ds(pl.multiple_of(pick(column[t], j) * width, width), width)

    def to_sum(t, n, group):
        lines = chain(n)[0]
        return remote(mine.at[t, lines, :], arrived.at[t, lines, :], sum_send.at[t, n],
                      sum_recv.at[t, n], dev(c, j, group))

    def to_back(t, n, group):
        lines = chain(n)[0]
        spot = result.at[lines, place(t)]
        return remote(spot, spot, back_send.at[t, n], back_recv.at[t, n], dev(c, j, group))

    def reduce(t):
        @pl.loop(0, 2 * SUBS)
        def _(n):
            lines, first, last, step = chain(n)
            mine[t, lines, :] = mine[t, lines, :] + got[t, lines, :]

            @pl.when(jnp.logical_not(first))
            def _():
                to_sum(t, n, s - step).wait_recv()
                mine[t, lines, :] = mine[t, lines, :] + arrived[t, lines, :]

            @pl.when(jnp.logical_not(last))
            def _():
                to_sum(t, n, s + step).start()

            @pl.when(last)
            def _():
                result[lines, place(t)] = (mine[t, lines, :] / total).astype(jnp.bfloat16)
                to_back(t, n, s - step).start()

    def finish(t):
        @pl.loop(0, 2 * SUBS)
        def _(n):
            lines, first, last, step = chain(n)

            @pl.when(jnp.logical_not(last))
            def _():
                to_back(t, n, s + step).wait_recv()

                @pl.when(jnp.logical_not(first))
                def _():
                    to_back(t, n, s - step).start()

        store(t).start()

    def store(t):
        return pltpu.make_async_copy(result.at[:, place(t)], out.at[:, place(t)], out_sem.at[t])

    grams(0)
    reduce(0)
    take_far(0)
    finish(0)
    for q in range(1, PARTS):
        take_far(q)
    take_near()
    grams(1)
    reduce(1)
    grams(2)
    reduce(2)
    finish(1)
    take_third()
    grams(3)
    reduce(3)
    finish(2)
    finish(3)

    for off in range(1, ns):
        stat_out(off).wait_send()
    swap.wait_send()

    @pl.when(has_far)
    def _():
        for q in range(PARTS):
            far(q).wait_send()

    @pl.when(has_near)
    def _():
        for q in range(PARTS):
            near(q).wait_send()

    @pl.when(c >= 1)
    def _():
        third().wait_send()

    @pl.when(relays)
    def _():
        for q in range(PARTS):
            passed(q).wait_send()

    for t in range(REACH):
        gave(t).wait_send()
        store(t).wait()

        @pl.loop(0, 2 * SUBS)
        def _(n):
            lines, first, last, step = chain(n)

            @pl.when(jnp.logical_not(last))
            def _():
                to_sum(t, n, s + step).wait_send()

            @pl.when(jnp.logical_not(first))
            def _():
                to_back(t, n, s - step).wait_send()


def per_device(nv, ns, dosages, window_end):
    rows, width = dosages.shape
    half = rows // 2
    dma = pltpu.SemaphoreType.DMA
    f32, bf16 = jnp.float32, jnp.bfloat16
    raw = pl.pallas_call(
        functools.partial(kernel, rows * ns, nv, ns),
        out_shape=jax.ShapeDtypeStruct((width, REACH * width), bf16),
        in_specs=[pl.BlockSpec(memory_space=pltpu.VMEM)],
        out_specs=pl.BlockSpec(memory_space=pl.ANY),
        scratch_shapes=[
            pltpu.VMEM((REACH + 1, half, width), bf16),
            pltpu.VMEM((2, width, half), bf16),
            pltpu.VMEM((half, width), bf16),
            pltpu.VMEM((ns, 8, width), f32),
            pltpu.VMEM((REACH, width, width), f32),
            pltpu.VMEM((REACH, width, width), f32),
            pltpu.VMEM((REACH, width, width), f32),
            pltpu.VMEM((REACH, width, width), f32),
            pltpu.VMEM((width, REACH * width), bf16),
            dma((ns,)), dma((ns,)), dma(()), dma(()),
            dma((PARTS,)), dma((PARTS,)), dma((PARTS,)), dma(()),
            dma((PARTS,)), dma((PARTS,)), dma(()), dma((REACH,)), dma((REACH,)),
            dma((REACH, 2 * SUBS)), dma((REACH, 2 * SUBS)),
            dma((REACH, 2 * SUBS)), dma((REACH, 2 * SUBS)), dma((REACH,)),
        ],
        compiler_params=pltpu.CompilerParams(
            collective_id=0, has_side_effects=True, vmem_limit_bytes=60 * 1024 * 1024
        ),
    )(dosages)
    columns = jnp.arange(REACH * width, dtype=jnp.int32)
    target = lax.axis_index("var") * width + columns
    keep = (columns[None, :] < width) | (target[None, :] <= window_end[:, None])
    return jnp.where(keep, raw, jnp.zeros((), bf16))


def solution(mesh):
    placed = (P("samp", "var"), P("var"))
    return jax.shard_map(
        functools.partial(per_device, mesh.shape["var"], mesh.shape["samp"]),
        mesh=mesh, in_specs=placed, out_specs=P("var", None), check_vma=False,
    )
```

time: 400 us -> 556 us (1.39)
  Pallas kernels: 0 us -> 552 us
  waiting for transfers between devices: 345 us -> 0 us
  between operations: 13.4 us -> 0.03 us
  matrix products: 10.8 us -> 0 us
  blocking collectives: 8.15 us -> 0 us
    pallas_call x0 -> x1, Pallas kernels: none -> 552 us  [per_device(): pl.pallas_call(functools.partial(kernel, rows * ns, nv, ns), out_shape=ja...]
    ppermute x3 -> x0, waiting for transfers between devices: 179 us -> none  [passed_along(): lax.ppermute(value, axis, [(source, source + steps) for source in range(f...]
    reduce_scatter x1 -> x0, waiting for transfers between devices: 121 us -> none  [per_device(): lax.psum_scatter(jnp.einsum('sa,sb->ab', standard, band, preferred_elemen...]
    all_gather x1 -> x0, waiting for transfers between devices: 44.7 us -> none  [per_device(): lax.all_gather(jnp.where(keep, mine / total, 0.0).astype(jnp.bfloat16), '...]
    dot_general x1 -> x0, matrix products: 10.8 us -> none  [per_device(): jnp.einsum('sa,sb->ab', standard, band, preferred_element_type=jnp.float32)]
    psum x1 -> x0, blocking collectives: 8.15 us -> none  [per_device(): lax.psum((jnp.sum(data, axis=0), jnp.sum(data * data, axis=0)), 'samp')]
  transfers between devices with their start and end apart: 5 -> 0, of which waited for: 5 -> 0; matrix products, arithmetic and copies ran while one was open for 0% -> 0% of each run, Pallas kernels for 0% -> 0%
where the time goes in v1:
time: 556 us
  Pallas kernels  552 us (99%)
    pallas_call x1, Pallas kernels, per_device(): pl.pallas_call(functools.partial(kernel, rows * ns, nv, ns), out_shape=ja...  552 us

profile of v1, /device:TPU:26, one launch (start us, length us, event | category | flops | bytes accessed | tf_op | source)
XLA Modules:
  0.0 555.9 jit_solution(5034105549016836414)
XLA Ops:
  0.0 0.0 copy-start
  0.0 551.9 %shard_map.28 = bf16[512,2048]{1,0:T(8,128)(2,1)} custom-call(bf16[4096,512]{1,0:T(8,128)(2,1)} %data.1), custom_call_target="tpu_custom_call" | custom-call | tf_op jit(solution)/shard_map/pallas_call | solution.py:330
  552.0 0.0 copy-done
  552.0 3.9 or_select_fusion
  (2 shorter events, 0.0 us)
Async XLA Ops:
  0.0 552.0 %copy-start = (s32[512]{0:T(512)S(1)}, s32[512]{0:T(512)}, u32[]{:S(2)}) copy-start(s32[512]{0:T(512)} %param.3) | copy-start | bytes 6148

commit v2 on v1

--- a/solution.py
+++ b/solution.py
@@ -11,6 +11,8 @@
 REACH = 4
 PARTS = 4
 SUBS = 4
+SLACK = 1
+PACE = 3
 
 
 def kernel(
@@ -113,7 +115,7 @@
     remote(other, x.at[1 - j], swap_send, swap_recv, dev(c, 1 - j, s)).wait_recv()
 
     def piece(slot, q):
-        return x.at[slot, pl.ds(q * part, part), :]
+        return x.at[slot, pl.ds(pl.multiple_of(q * part, part), part), :]
 
     def near(q):
         return remote(piece(0, q), piece(2, q), near_send.at[q], near_recv.at[q], dev(c - 1, j, s))
@@ -146,15 +148,20 @@
     def _():
         third().start()
 
-    def take_far(q):
-        @pl.when(c + 2 < chips)
-        def _():
-            remote(piece(0, q), piece(4, q), far_send.at[q], far_recv.at[q],
-                   dev(c + 2, j, s)).wait_recv()
-
+    def far_here(q):
+        return remote(piece(0, q), piece(4, q), far_send.at[q], far_recv.at[q], dev(c + 2, j, s))
+
+    def relay(q):
         @pl.when(relays)
         def _():
+            far_here(q).wait_recv()
             passed(q).start()
+
+    def take_far():
+        @pl.when((c + 2 < chips) & odd)
+        def _():
+            for q in range(PARTS):
+                far_here(q).wait_recv()
 
     def take_near():
         @pl.when(c + 1 < chips)
@@ -176,7 +183,6 @@
 
     side = min(256, width)
     slots = ((0, 1), (1, 2), (2, 4), (3, 3))
-    column = ((0, 0), (1, 1), (2, 3), (3, 2))
 
     def pick(pair, r):
         return pair[0] + r * (pair[1] - pair[0])
@@ -184,29 +190,36 @@
     def product(t, r, into):
         slot = pick(slots[t], r)
 
-        @pl.loop(0, (width // side) ** 2)
+        @pl.loop(0, width // side)
         def _(i):
-            top = pl.multiple_of((i // (width // side)) * side, side)
-            left = pl.multiple_of((i % (width // side)) * side, side)
-            into[t, pl.ds(top, side), pl.ds(left, side)] = jnp.dot(
-                xt[r, pl.ds(top, side), :], x[slot, :, pl.ds(left, side)],
-                preferred_element_type=jnp.float32,
+            left = pl.multiple_of(i * side, side)
+            into[t, :, pl.ds(left, side)] = jnp.dot(
+                xt[r], x[slot, :, pl.ds(left, side)], preferred_element_type=jnp.float32
             )
 
     def gave(t):
         return remote(give.at[t], got.at[t], give_send.at[t], give_recv.at[t], dev(c, 1 - j, s))
 
-    def grams(t):
-        product(t, 1 - j, give)
-        gave(t).start()
-        product(t, j, mine)
-        gave(t).wait_recv()
+    def grams(steps):
+        for t, only in steps:
+            @pl.when(True if only is None else 1 - j == only)
+            def _():
+                product(t, 1 - j, give)
+                gave(t).start()
+        for t, only in steps:
+            @pl.when(True if only is None else j == only)
+            def _():
+                product(t, j, mine)
+        for t, only in steps:
+            @pl.when(True if only is None else j == only)
+            def _():
+                gave(t).wait_recv()
 
     block = width // 2 // SUBS
 
     def chain(n):
-        way = n % 2
-        u = n // 2
+        way = n // SUBS
+        u = n % SUBS
         lines = pl.ds(pl.multiple_of(way * (width // 2) + u * block, block), block)
         first = s == way * (ns - 1)
         last = s == (1 - way) * (ns - 1)
@@ -214,7 +227,8 @@
         return lines, first, last, step
 
     def place(t):
-        return pl.ds(pl.multiple_of(pick(column[t], j) * width, width), width)
+        k = jnp.where((j == 1) & (t >= 2), 5 - t, t)
+        return pl.ds(pl.multiple_of(k * width, width), width)
 
     def to_sum(t, n, group):
         lines = chain(n)[0]
@@ -226,61 +240,79 @@
         spot = result.at[lines, place(t)]
         return remote(spot, spot, back_send.at[t, n], back_recv.at[t, n], dev(c, j, group))
 
-    def reduce(t):
-        @pl.loop(0, 2 * SUBS)
-        def _(n):
-            lines, first, last, step = chain(n)
-            mine[t, lines, :] = mine[t, lines, :] + got[t, lines, :]
+    def reduce(t, n):
+        lines, first, last, step = chain(n)
+        mine[t, lines, :] = mine[t, lines, :] + got[t, lines, :]
+
+        @pl.when(jnp.logical_not(first))
+        def _():
+            to_sum(t, n, s - step).wait_recv()
+            mine[t, lines, :] = mine[t, lines, :] + arrived[t, lines, :]
+
+        @pl.when(jnp.logical_not(last))
+        def _():
+            to_sum(t, n, s + step).start()
+
+        @pl.when(last)
+        def _():
+            result[lines, place(t)] = (mine[t, lines, :] / total).astype(jnp.bfloat16)
+            to_back(t, n, s - step).start()
+
+    def bring(t, n):
+        lines, first, last, step = chain(n)
+
+        @pl.when(jnp.logical_not(last))
+        def _():
+            to_back(t, n, s + step).wait_recv()
 
             @pl.when(jnp.logical_not(first))
             def _():
-                to_sum(t, n, s - step).wait_recv()
-                mine[t, lines, :] = mine[t, lines, :] + arrived[t, lines, :]
-
-            @pl.when(jnp.logical_not(last))
-            def _():
-                to_sum(t, n, s + step).start()
-
-            @pl.when(last)
-            def _():
-                result[lines, place(t)] = (mine[t, lines, :] / total).astype(jnp.bfloat16)
                 to_back(t, n, s - step).start()
 
-    def finish(t):
-        @pl.loop(0, 2 * SUBS)
-        def _(n):
-            lines, first, last, step = chain(n)
-
-            @pl.when(jnp.logical_not(last))
-            def _():
-                to_back(t, n, s + step).wait_recv()
-
-                @pl.when(jnp.logical_not(first))
-                def _():
-                    to_back(t, n, s - step).start()
-
-        store(t).start()
+    def walk(start, count, beside=None):
+        pieces = count * SUBS
+        ends = ns - 1
+
+        @pl.loop(0, pieces + 2 * ends + SLACK)
+        def _(turn):
+            for way in range(2):
+                hops = s if way == 0 else ends - s
+                for u, body in (
+                    (turn - hops, reduce),
+                    (turn - (2 * ends - hops + SLACK), bring),
+                ):
+                    @pl.when((u >= 0) & (u < pieces))
+                    def _():
+                        body(start + u // SUBS, way * SUBS + u % SUBS)
+            if beside is not None:
+                beside(turn)
 
     def store(t):
         return pltpu.make_async_copy(result.at[:, place(t)], out.at[:, place(t)], out_sem.at[t])
 
-    grams(0)
-    reduce(0)
-    take_far(0)
-    finish(0)
-    for q in range(1, PARTS):
-        take_far(q)
+    shortest = SUBS + 2 * (ns - 1) + SLACK
+    inside = len([q for q in range(PARTS) if PACE * q + 1 < shortest])
+
+    def beside(turn):
+        @pl.when((turn % PACE == 1) & (turn // PACE < inside))
+        def _():
+            relay(turn // PACE)
+
+    grams(((0, None), (1, 0)))
+    walk(0, 2 - j, beside)
+    for q in range(inside, PARTS):
+        relay(q)
+    store(0).start()
     take_near()
-    grams(1)
-    reduce(1)
-    grams(2)
-    reduce(2)
-    finish(1)
+    take_far()
+    grams(((1, 1), (2, None)))
+    walk(2 - j, 1 + j)
+    store(1).start()
+    store(2).start()
     take_third()
-    grams(3)
-    reduce(3)
-    finish(2)
-    finish(3)
+    grams(((3, None),))
+    walk(3, 1)
+    store(3).start()
 
     for off in range(1, ns):
         stat_out(off).wait_send()

time: 556 us -> 203 us (0.37)
  Pallas kernels: 552 us -> 198 us
    pallas_call x1, Pallas kernels: 552 us -> 198 us  [per_device(): pl.pallas_call(functools.partial(kernel, rows * ns, nv, ns), out_shape=ja...]
where the time goes in v2:
time: 203 us; the launch traced here: 202 us
  Pallas kernels  198 us (98%)
  other arithmetic  3.92 us (2%)
    pallas_call x1, Pallas kernels, per_device(): pl.pallas_call(functools.partial(kernel, rows * ns, nv, ns), out_shape=ja...  198 us

profile of v2, /device:TPU:26, one launch (start us, length us, event | category | flops | bytes accessed | tf_op | source)
XLA Modules:
  0.0 202.3 jit_solution(7395135917462913600)
XLA Ops:
  0.0 0.0 copy-start
  0.0 198.4 %shard_map.28 = bf16[512,2048]{1,0:T(8,128)(2,1)} custom-call(bf16[4096,512]{1,0:T(8,128)(2,1)} %data.1), custom_call_target="tpu_custom_call" | custom-call | tf_op jit(solution)/shard_map/pallas_call | solution.py:362
  198.4 0.0 copy-done
  198.4 3.9 %or_select_fusion = bf16[512,2048]{1,0:T(8,128)(2,1)} fusion(bf16[512,2048]{1,0:T(8,128)(2,1)} %shard_map.28, s32[2048]{0:T(1024)S(1)} %iota_add_fusion, s32[512]{0:T(512)S(1)} %copy-done, pred[2048]{0:T(1024)(128)(4,1)S(1)} %iota_compare_fusion), kind=kLoop, calls=%fused_computation | loop fusion | flops 3145728 | bytes 4206592 | tf_op jit(solution)/shard_map/jit(_where)/select_n | solution.py:390
  (2 shorter events, 0.0 us)
Async XLA Ops:
  0.0 198.4 %copy-start = (s32[512]{0:T(512)S(1)}, s32[512]{0:T(512)}, u32[]{:S(2)}) copy-start(s32[512]{0:T(512)} %param.3) | copy-start | bytes 6148

commit v3 on v2

--- a/solution.py
+++ b/solution.py
@@ -10,9 +10,9 @@
 MESH = pl.DeviceIdType.MESH
 REACH = 4
 PARTS = 4
-SUBS = 4
-SLACK = 1
-PACE = 3
+SUBS = 8
+SLACK = 4
+LAG = 3
 
 
 def kernel(
@@ -271,12 +271,12 @@
 
     def walk(start, count, beside=None):
         pieces = count * SUBS
-        ends = ns - 1
+        ends = LAG * (ns - 1)
 
         @pl.loop(0, pieces + 2 * ends + SLACK)
         def _(turn):
             for way in range(2):
-                hops = s if way == 0 else ends - s
+                hops = LAG * (s if way == 0 else ns - 1 - s)
                 for u, body in (
                     (turn - hops, reduce),
                     (turn - (2 * ends - hops + SLACK), bring),
@@ -290,13 +290,14 @@
     def store(t):
         return pltpu.make_async_copy(result.at[:, place(t)], out.at[:, place(t)], out_sem.at[t])
 
-    shortest = SUBS + 2 * (ns - 1) + SLACK
-    inside = len([q for q in range(PARTS) if PACE * q + 1 < shortest])
+    shortest = SUBS + 2 * LAG * (ns - 1) + SLACK
+    pace = max(1, shortest // PARTS)
+    inside = len([q for q in range(PARTS) if pace * q < shortest])
 
     def beside(turn):
-        @pl.when((turn % PACE == 1) & (turn // PACE < inside))
-        def _():
-            relay(turn // PACE)
+        @pl.when((turn % pace == 0) & (turn // pace < inside))
+        def _():
+            relay(turn // pace)
 
     grams(((0, None), (1, 0)))
     walk(0, 2 - j, beside)
@@ -304,14 +305,14 @@
         relay(q)
     store(0).start()
     take_near()
+    grams(((1, 1), (2, 0)))
+    walk(2 - j, 1)
+    store(1).start()
     take_far()
-    grams(((1, 1), (2, None)))
-    walk(2 - j, 1 + j)
-    store(1).start()
+    take_third()
+    grams(((2, 1), (3, None)))
+    walk(3 - j, 1 + j)
     store(2).start()
-    take_third()
-    grams(((3, None),))
-    walk(3, 1)
     store(3).start()
 
     for off in range(1, ns):

time: 203 us -> 156 us (0.77)
  the two profiles are of different devices: /device:TPU:26 before, /device:TPU:3 now
where the time goes in v3:
time: 156 us
  Pallas kernels  152 us (97%)
  other arithmetic  3.92 us (3%)
    pallas_call x1, Pallas kernels, per_device(): pl.pallas_call(functools.partial(kernel, rows * ns, nv, ns), out_shape=ja...  152 us
    select_n x1, other arithmetic, per_device(): return jnp.where(keep, raw, jnp.zeros((), bf16))  3.91 us

profile of v3, /device:TPU:3, one launch (start us, length us, event | category | flops | bytes accessed | tf_op | source)
XLA Modules:
  0.0 155.7 jit_solution(2411908089563738964)
XLA Ops:
  0.0 0.0 copy-start
  0.0 151.8 %shard_map.28 = bf16[512,2048]{1,0:T(8,128)(2,1)} custom-call(bf16[4096,512]{1,0:T(8,128)(2,1)} %data.1), custom_call_target="tpu_custom_call" | custom-call | tf_op jit(solution)/shard_map/pallas_call | solution.py:363
  151.8 0.0 copy-done
  151.8 3.9 %or_select_fusion = bf16[512,2048]{1,0:T(8,128)(2,1)} fusion(bf16[512,2048]{1,0:T(8,128)(2,1)} %shard_map.28, s32[2048]{0:T(1024)S(1)} %iota_add_fusion, s32[512]{0:T(512)S(1)} %copy-done, pred[2048]{0:T(1024)(128)(4,1)S(1)} %iota_compare_fusion), kind=kLoop, calls=%fused_computation | loop fusion | flops 3145728 | bytes 4206592 | tf_op jit(solution)/shard_map/jit(_where)/select_n | solution.py:391
  (2 shorter events, 0.0 us)
Async XLA Ops:
  0.0 151.8 %copy-start = (s32[512]{0:T(512)S(1)}, s32[512]{0:T(512)}, u32[]{:S(2)}) copy-start(s32[512]{0:T(512)} %param.3) | copy-start | bytes 6148

commit v4 on v3

--- a/solution.py
+++ b/solution.py
@@ -104,6 +104,46 @@
         at = pl.multiple_of(i * tile, tile)
         x[j, pl.ds(at, tile), :] = standard(j * half + at)
 
+    def piece(slot, q):
+        return x.at[slot, pl.ds(pl.multiple_of(q * part, part), part), :]
+
+    def near(q):
+        return remote(piece(0, q), piece(2, q), near_send.at[q], near_recv.at[q], dev(c - 1, j, s))
+
+    def far(q):
+        return remote(piece(0, q), piece(4, q), far_send.at[q], far_recv.at[q], dev(c - 2, j, s))
+
+    def passed(q):
+        return remote(piece(4, q), piece(2, q), pass_send.at[q], near_recv.at[q], dev(c + 1, j, s))
+
+    def third():
+        return remote(x.at[1], x.at[3], third_send, third_recv, dev(c - 1, j, s))
+
+    odd = c % 2 == 1
+    has_far = c >= 2
+    has_near = (c >= 1) & odd
+    relays = (c % 2 == 0) & (c + 2 < chips)
+
+    def first_block(core):
+        @pl.when(has_far & (j == core))
+        def _():
+            for q in range(PARTS):
+                far(q).start()
+
+        @pl.when(has_near & (j == core))
+        def _():
+            for q in range(PARTS):
+                near(q).start()
+
+    first_block(0)
+    remote(other, x.at[1 - j], swap_send, swap_recv, dev(c, 1 - j, s)).wait_recv()
+
+    first_block(1)
+
+    @pl.when(c >= 1)
+    def _():
+        third().start()
+
     for slot, reach in ((2, 1), (3, 1), (4, 2)):
         @pl.when(c + reach >= chips)
         def _():
@@ -111,42 +151,6 @@
             def _(i):
                 at = pl.multiple_of(i * tile, tile)
                 x[slot, pl.ds(at, tile), :] = jnp.zeros((tile, width), jnp.bfloat16)
-
-    remote(other, x.at[1 - j], swap_send, swap_recv, dev(c, 1 - j, s)).wait_recv()
-
-    def piece(slot, q):
-        return x.at[slot, pl.ds(pl.multiple_of(q * part, part), part), :]
-
-    def near(q):
-        return remote(piece(0, q), piece(2, q), near_send.at[q], near_recv.at[q], dev(c - 1, j, s))
-
-    def far(q):
-        return remote(piece(0, q), piece(4, q), far_send.at[q], far_recv.at[q], dev(c - 2, j, s))
-
-    def passed(q):
-        return remote(piece(4, q), piece(2, q), pass_send.at[q], near_recv.at[q], dev(c + 1, j, s))
-
-    def third():
-        return remote(x.at[1], x.at[3], third_send, third_recv, dev(c - 1, j, s))
-
-    odd = c % 2 == 1
-    has_far = c >= 2
-    has_near = (c >= 1) & odd
-    relays = (c % 2 == 0) & (c + 2 < chips)
-
-    @pl.when(has_far)
-    def _():
-        for q in range(PARTS):
-            far(q).start()
-
-    @pl.when(has_near)
-    def _():
-        for q in range(PARTS):
-            near(q).start()
-
-    @pl.when(c >= 1)
-    def _():
-        third().start()
 
     def far_here(q):
         return remote(piece(0, q), piece(4, q), far_send.at[q], far_recv.at[q], dev(c + 2, j, s))

time: 156 us -> 153 us (0.981)
  the two profiles are of different devices: /device:TPU:3 before, /device:TPU:1 now
where the time goes in v4:
time: 153 us
  Pallas kernels  149 us (97%)
  other arithmetic  3.92 us (3%)
    pallas_call x1, Pallas kernels, per_device(): pl.pallas_call(functools.partial(kernel, rows * ns, nv, ns), out_shape=ja...  149 us
    select_n x1, other arithmetic, per_device(): return jnp.where(keep, raw, jnp.zeros((), bf16))  3.91 us

profile of v4, /device:TPU:1, one launch (start us, length us, event | category | flops | bytes accessed | tf_op | source)
XLA Modules:
  0.0 153.2 jit_solution(13106131923819883932)
XLA Ops:
  0.0 0.0 copy-start
  0.0 149.3 %shard_map.28 = bf16[512,2048]{1,0:T(8,128)(2,1)} custom-call(bf16[4096,512]{1,0:T(8,128)(2,1)} %data.1), custom_call_target="tpu_custom_call" | custom-call | tf_op jit(solution)/shard_map/pallas_call | solution.py:367
  149.3 0.0 copy-done
  149.3 3.9 %or_select_fusion = bf16[512,2048]{1,0:T(8,128)(2,1)} fusion(bf16[512,2048]{1,0:T(8,128)(2,1)} %shard_map.28, s32[2048]{0:T(1024)S(1)} %iota_add_fusion, s32[512]{0:T(512)S(1)} %copy-done, pred[2048]{0:T(1024)(128)(4,1)S(1)} %iota_compare_fusion), kind=kLoop, calls=%fused_computation | loop fusion | flops 3145728 | bytes 4206592 | tf_op jit(solution)/shard_map/jit(_where)/select_n | solution.py:395
  (2 shorter events, 0.0 us)
Async XLA Ops:
  0.0 149.3 %copy-start = (s32[512]{0:T(512)S(1)}, s32[512]{0:T(512)}, u32[]{:S(2)}) copy-start(s32[512]{0:T(512)} %param.3) | copy-start | bytes 6148
